TPU v7x, 32 devices: a whole 2x2x4 slice. The times are simulated.
32 devices in a mesh: recv: 4 (over x, core), send: 8 (over z, y).
Axes of the slice: x: 2, y: 2, z: 4, core: 2. Of those that a mesh axis runs over, the one named last changes fastest.
Arguments:
- latent: float32 [4096, 512], P(('recv', 'send')), may hold values from -6 to 6
- edge_feat: float32 [32768, 512], P(('recv', 'send')), may hold values from -6 to 6
- senders: int32 [32768], P(('recv', 'send')), may hold values from 0 to 4095, as said below
- receivers: int32 [32768], P(('recv', 'send')), may hold values from 0 to 4095, as said below
- live_blocks: int32 [32], P(('recv', 'send')), may hold values from 1 to 8, as said below
- cotangent: float32 [32768, 512], P(('recv', 'send')), may hold values from -6 to 6
- w_first: float32 [1536, 512], replicated, may hold values from -0.15625 to 0.15625
- first_bias: float32 [512], replicated, may hold values from -3 to 3
- w_second: float32 [512, 512], replicated, may hold values from -0.25 to 0.25
- second_bias: float32 [512], replicated, may hold values from -3 to 3
- norm_gain: float32 [512], replicated, may hold values from 0.1 to 1.9
Outputs:
- edge_grad: float32 [32768, 512], P(('recv', 'send'))
- sender_grad: float32 [4096, 512], P(('recv', 'send'))
- receiver_grad: float32 [4096, 512], P(('recv', 'send'))
- first_weight_grad: float32 [1536, 512], replicated
- second_weight_grad: float32 [512, 512], replicated
- bias_grads: float32 [4, 512], replicated
Inputs may be any that keep to these rules, and one draw needn't show every extreme that they name: `receivers`: slot e lies in tile t = e // 1024; with i = t // (devices along send), its receiver r has (r // 128) // (devices along send) = i. The first two slots of every tile name the last and the first node of that receiver block. `senders`: slot e lies in tile t = e // 1024; with j = t mod (devices along send), its sender s has (s // 128) mod (devices along send) = j. The first two slots of every tile name the last and the first node of that sender block. Tile t's first 128 * live_blocks[t] slots hold edges; its other slots are padding whose cotangent is ignored. Some tile is full in every draw.
All inputs are finite; a program needn't handle non-finite values.
Results may differ from a plain program's by a relative error of at most 0.0001.
Values sent between devices are 32-bit elements; how exact they have to be, the bound alone decides.
A program may use at most 128 MiB of HBM per device.

v0:
```python
import math

import jax
import jax.numpy as jnp
from jax import lax
from jax.sharding import PartitionSpec as P

norm_eps = 1e-05
block_rows = 128


def exact_dot(left, right):
    return jnp.dot(left, right, precision=lax.Precision.HIGHEST, preferred_element_type=jnp.float32)


def outer_sum(left, right):
    return lax.dot_general(
        left,
        right,
        (((0,), (0,)), ((), ())),
        precision=lax.Precision.HIGHEST,
        preferred_element_type=jnp.float32,
    )


def trans_dot(left, right):
    return lax.dot_general(
        left,
        right,
        (((1,), (1,)), ((), ())),
        precision=lax.Precision.HIGHEST,
        preferred_element_type=jnp.float32,
    )


def shards(
    latent,
    edge_feat,
    senders,
    receivers,
    live_blocks,
    cotangent,
    w_first,
    first_bias,
    w_second,
    second_bias,
    norm_gain,
):
    model_width = latent.shape[1]
    node_rows = latent.shape[0]
    slot_count = edge_feat.shape[0]
    recv_count = lax.axis_size("recv")
    send_count = lax.axis_size("send")
    recv_index = lax.axis_index("recv")
    recv_local = receivers - recv_index * (send_count * node_rows)
    piece_index = senders // node_rows
    send_local = piece_index // send_count * node_rows + senders % node_rows
    live_limit = block_rows * live_blocks[0]
    sender_table = lax.all_gather(latent, "recv", axis=0, tiled=True)
    receiver_table = lax.all_gather(latent, "send", axis=0, tiled=True)
    first_rows = 3 * model_width

    def block_work(accs, edge_rows, grad_rows, sender_rows, recv_ids):
        first_grad, second_grad, hidden_bias, outer_bias, gain_grad, offset_grad, receiver_acc = (
            accs
        )
        receiver_rows = jnp.take(receiver_table, recv_ids, axis=0)
        joined = jnp.concatenate([edge_rows, sender_rows, receiver_rows], axis=1)
        hidden = exact_dot(joined, w_first) + first_bias
        sigmoid_hidden = jax.nn.sigmoid(hidden)
        active = hidden * sigmoid_hidden
        output = exact_dot(active, w_second) + second_bias
        centred = output - jnp.mean(output, axis=1, keepdims=True)
        inv_std = lax.rsqrt(jnp.mean(centred * centred, axis=1, keepdims=True) + norm_eps)
        normed = centred * inv_std
        scaled = grad_rows * norm_gain
        norm_grad = inv_std * (
            scaled
            - jnp.mean(scaled, axis=1, keepdims=True)
            - normed * jnp.mean(scaled * normed, axis=1, keepdims=True)
        )
        hidden_grad = (
            trans_dot(norm_grad, w_second)
            * sigmoid_hidden
            * (1.0 + hidden * (1.0 - sigmoid_hidden))
        )
        first_grad = first_grad + outer_sum(joined, hidden_grad)
        second_grad = second_grad + outer_sum(active, norm_grad)
        hidden_bias = hidden_bias + jnp.sum(hidden_grad, axis=0)
        outer_bias = outer_bias + jnp.sum(norm_grad, axis=0)
        gain_grad = gain_grad + jnp.sum(grad_rows * normed, axis=0)
        offset_grad = offset_grad + jnp.sum(grad_rows, axis=0)
        joined_grad = trans_dot(hidden_grad, w_first)
        edge_part = joined_grad[:, :model_width]
        sender_part = joined_grad[:, model_width : 2 * model_width]
        receiver_acc = receiver_acc.at[recv_ids].add(joined_grad[:, 2 * model_width :])
        accs = (
            first_grad,
            second_grad,
            hidden_bias,
            outer_bias,
            gain_grad,
            offset_grad,
            receiver_acc,
        )
        return (accs, grad_rows + edge_part, sender_part)

    def local_block(offset):
        edge_rows = lax.dynamic_slice_in_dim(edge_feat, offset, block_rows, 0)
        position = offset + jnp.arange(block_rows, dtype=jnp.int32)
        live_rows = (position < live_limit).astype(jnp.float32)[:, None]
        grad_rows = lax.dynamic_slice_in_dim(cotangent, offset, block_rows, 0) * live_rows
        send_ids = lax.dynamic_slice_in_dim(send_local, offset, block_rows, 0)
        recv_ids = lax.dynamic_slice_in_dim(recv_local, offset, block_rows, 0)
        sender_rows = jnp.take(sender_table, send_ids, axis=0)
        return (edge_rows, grad_rows, send_ids, recv_ids, sender_rows)

    feature_zeros = jnp.zeros((model_width,), jnp.float32)
    accs = (
        jnp.zeros((first_rows, model_width), jnp.float32),
        jnp.zeros((model_width, model_width), jnp.float32),
        feature_zeros,
        feature_zeros,
        feature_zeros,
        feature_zeros,
        jnp.zeros(receiver_table.shape, jnp.float32),
    )
    sender_acc = jnp.zeros(sender_table.shape, jnp.float32)
    edge_out = jnp.zeros(edge_feat.shape, jnp.float32)

    def own_step(block, carried):
        accs_now, sender_now, edge_now = carried
        offset = block * block_rows
        edge_rows, grad_rows, send_ids, recv_ids, sender_rows = local_block(offset)
        accs_now, edge_block, sender_block = block_work(
            accs_now, edge_rows, grad_rows, sender_rows, recv_ids
        )
        sender_now = sender_now.at[send_ids].add(sender_block)
        edge_now = lax.dynamic_update_slice_in_dim(edge_now, edge_block, offset, 0)
        return (accs_now, sender_now, edge_now)

    accs, sender_acc, edge_out = lax.fori_loop(
        0, live_blocks[0], own_step, (accs, sender_acc, edge_out)
    )
    first_grad, second_grad, hidden_bias, outer_bias, gain_grad, offset_grad, receiver_acc = accs
    sender_grad = lax.psum_scatter(sender_acc, "recv", scatter_dimension=0, tiled=True)
    receiver_grad = lax.psum_scatter(receiver_acc, "send", scatter_dimension=0, tiled=True)
    small_grads = jnp.stack([hidden_bias, outer_bias, gain_grad, offset_grad])
    first_total, second_total, small_total = lax.psum(
        (first_grad, second_grad, small_grads), ("recv", "send")
    )
    factor = 1.0 / math.sqrt(slot_count * recv_count * send_count)
    return (
        edge_out,
        sender_grad,
        receiver_grad,
        first_total * factor,
        second_total * factor,
        small_total * factor,
    )


def solution(mesh):
    return jax.shard_map(
        shards,
        mesh=mesh,
        in_specs=(
            P(("recv", "send"), None),
            P(("recv", "send"), None),
            P(("recv", "send")),
            P(("recv", "send")),
            P(("recv", "send")),
            P(("recv", "send"), None),
            P(),
            P(),
            P(),
            P(),
            P(),
        ),
        out_specs=(
            P(("recv", "send"), None),
            P(("recv", "send"), None),
            P(("recv", "send"), None),
            P(),
            P(),
            P(),
        ),
        check_vma=False,
    )
```

profile of v0, /device:TPU:0, one launch (start us, length us, event | category | flops | bytes accessed | tf_op | source)
XLA Modules:
  0.0 649.5 jit_solution(7967292514408695948)
XLA Ops:
  7.9 0.7 all-gather.5.cloned.1.call-update
  9.3 0.7 fusion.16
  10.1 18.9 %all-gather.3.cloned.1.call-done = f32[512,512]{1,0:T(8,128)} async-done(((f32[128,512]{1,0:T(8,128)}), f32[512,512]{1,0:T(8,128)}) %all-gather.3.cloned.1.call-update) | async-done | bytes 1048592 | tf_op jit(solution)/shard_map/all_gather | solution.py:59
  29.0 51.5 %all-gather.5.cloned.1.call-done = f32[1024,512]{1,0:T(8,128)} async-done(((f32[128,512]{1,0:T(8,128)}), f32[1024,512]{1,0:T(8,128)}) %all-gather.5.cloned.1.call-update) | async-done | bytes 2097168 | tf_op jit(solution)/shard_map/all_gather | solution.py:60
  80.5 1.1 broadcast.80.clone
  81.6 1.1 broadcast.80
  82.7 1.6 broadcast.81.clone
  84.3 1.6 broadcast.81
  86.0 2.1 broadcast_in_dim.38
  88.0 1.0 copy-done
  89.0 39.9 %while.26 = (s32[]{:T(128)}, f32[1536,512]{1,0:T(8,128)}, f32[512,512]{1,0:T(8,128)}, f32[512]{0:T(512)S(1)}, f32[512]{0:T(512)S(1)}, /*index=5*/f32[512]{0:T(51...) while((s32[]{:T(128)}, f32[1536,512]{1,0:T(8,128)}, ...), condition=%wide.region_11.12_spmd, body=%wide.region_0.11_spmd.sunk | while | flops 4836823040 | bytes 37814700 | solution.py:142
  89.8 3.2 gather_fusion
  93.0 1.0 broadcast_select_fusion.4
  94.0 2.9 gather_fusion.1
  96.9 1.1 broadcast_select_fusion.5
  98.1 1.9 convolution_add_fusion.7
  100.0 0.8 fusion.59
  101.0 1.2 multiply_reduce_fusion.7
  102.3 1.1 fusion.60
  103.4 1.2 fusion.61
  104.7 3.2 convolution_add_fusion.9
  107.9 4.2 fusion.62
  112.1 4.0 scatter_custom_fusion.11
  116.1 1.8 fusion.63
  117.9 4.7 scatter_custom_fusion.10
  122.6 5.6 convolution_add_fusion.8
  130.1 312.5 %psum.23 = f32[4,512]{1,0:T(4,128)S(1)} all-reduce(f32[4,512]{1,0:T(4,128)S(1)} %pad_maximum_fusion.3), channel_id=1, replica_groups=mesh['recv'=4,'send'=8] {'recv','send'}, use_global_device_ids=true, to_apply=%region_16.17 | all-reduce | flops 2048 | bytes 16384 | tf_op jit(solution)/shard_map/psum | solution.py:149
  443.2 100.9 %all-reduce.3.cloned.1.call-done = (f32[1536,512]{1,0:T(8,128)}, f32[512,512]{1,0:T(8,128)}) async-done(((f32[1536,512]{1,0:T(8,128)}, f32[512,512]{1,0:T(8,128)}), (f32[1536,512]{1,0:T(8,128)}, f32[512,512]{1,0:T(8,128)})) %all-reduce.3.cloned.1.call-update) | async-done | bytes 4194320 | tf_op jit(solution)/shard_map/psum | solution.py:149
  544.1 2.3 broadcast_multiply_fusion.4
  546.4 3.9 broadcast_multiply_fusion.3
  550.3 20.5 %reduce-scatter.3.cloned.1.call-done = f32[128,512]{1,0:T(8,128)} async-done(((f32[512,512]{1,0:T(8,128)}), f32[128,512]{1,0:T(8,128)}) %reduce-scatter.3.cloned.1.call-update) | async-done | bytes 262160 | tf_op jit(solution)/shard_map/reduce_scatter | solution.py:146
  570.9 72.1 %reduce-scatter.5.cloned.1.call-done = f32[128,512]{1,0:T(8,128)} async-done(((f32[1024,512]{1,0:T(8,128)}), f32[128,512]{1,0:T(8,128)}) %reduce-scatter.5.cloned.1.call-update) | async-done | bytes 262160 | tf_op jit(solution)/shard_map/reduce_scatter | solution.py:147
  (43 shorter events, 3.0 us)
Async XLA Ops:
  7.2 21.8 %all-gather.3.cloned.1.call-start = ((), (), s32[]{:S(2)}) async-start(), calls=%async_computation.2 | async-start | bytes 1310720 | tf_op jit(solution)/shard_map/all_gather | solution.py:59
  7.9 72.6 %all-gather.5.cloned.1.call-start = ((), (), s32[]{:S(2)}) async-start(), calls=%async_computation.3 | async-start | bytes 2359296 | tf_op jit(solution)/shard_map/all_gather | solution.py:60
  8.6 535.4 %all-reduce.3.cloned.1.call-start = ((), (), s32[]{:S(2)}) async-start(), calls=%async_computation.6 | async-start | bytes 8388608 | tf_op jit(solution)/shard_map/psum | solution.py:149
  84.3 3.7 copy-start.5
  84.3 3.7 copy-start.6
  84.3 3.7 copy-start.7
  86.0 3.0 copy-start
  94.0 5.9 copy-start.2
  98.1 1.9 copy-start.3
  98.1 1.9 copy-start.4
  98.1 1.9 copy-start.1
  128.9 442.0 %reduce-scatter.3.cloned.1.call-start = ((), (), s32[]{:S(2)}) async-start(), calls=%async_computation.4 | async-start | bytes 1310720 | tf_op jit(solution)/shard_map/reduce_scatter | solution.py:146
  129.5 513.5 %reduce-scatter.5.cloned.1.call-start = ((), (), s32[]{:S(2)}) async-start(), calls=%async_computation.5 | async-start | bytes 2359296 | tf_op jit(solution)/shard_map/reduce_scatter | solution.py:147
Sparse Core Ops, SparseCore 0:
  9.6 19.4 all-gather.2
  31.1 49.2 all-gather.4
  129.0 415.0 all-reduce.2
  547.0 23.7 reduce-scatter.2
  575.2 67.7 reduce-scatter.4
where the time goes:
time: 653 us; the launch traced here: 650 us
  blocking collectives  312 us (48%)
  waiting for transfers between devices  266 us (41%)
  other arithmetic  22.9 us (4%)
  matrix products  17 us (3%)
  local copies, waits for them, and re-layouts  14.6 us (2%)
  between operations  14.5 us (2%)
    psum x1, blocking collectives, shards(): lax.psum((first_grad, second_grad, small_grads), ('recv', 'send'))  312 us
    psum x1, waiting for transfers between devices, shards(): lax.psum((first_grad, second_grad, small_grads), ('recv', 'send'))  101 us
    reduce_scatter x1, waiting for transfers between devices, shards(): lax.psum_scatter(receiver_acc, 'send', scatter_dimension=0, tiled=True)  72.1 us
    all_gather x1, waiting for transfers between devices, shards(): receiver_table = lax.all_gather(latent, 'send', axis=0, tiled=True)  51.5 us
    reduce_scatter x1, waiting for transfers between devices, shards(): lax.psum_scatter(sender_acc, 'recv', scatter_dimension=0, tiled=True)  20.5 us
    all_gather x1, waiting for transfers between devices, shards(): sender_table = lax.all_gather(latent, 'recv', axis=0, tiled=True)  18.9 us
  transfers between devices with their start and end apart: 5, of which 5 were waited for; matrix products, arithmetic and copies ran while one was open for 1% of the time, Pallas kernels for 0%

commit v1 on v0

v1 whole, which is shorter than its diff:
```python
import functools
import math

import jax
import jax.numpy as jnp
from jax import lax
from jax.experimental import pallas as pl
from jax.experimental.pallas import tpu as pltpu
from jax.sharding import PartitionSpec as P

norm_eps = 1e-05
block_rows = 128
step_rows = 256
MESH = pl.DeviceIdType.MESH
NN = (((1,), (0,)), ((), ()))
NT = (((1,), (1,)), ((), ()))
TN = (((0,), (0,)), ((), ()))


def split(value):
    high = value.astype(jnp.bfloat16)
    low = (value - high.astype(jnp.float32)).astype(jnp.bfloat16)
    return high, low


def mm(left, right, dims):
    return lax.dot_general(left, right, dims, preferred_element_type=jnp.float32)


def dot3(left, right, dims):
    return mm(left[0], right[0], dims) + mm(left[0], right[1], dims) + mm(left[1], right[0], dims)


def dot2(exact, right):
    return mm(exact, right[0], NN) + mm(exact, right[1], NN)


def bits_of(count):
    return max(count.bit_length() - 1, 0)


def my_bit(axis, bit):
    return (lax.axis_index(axis) // (1 << bit)) % 2


def partner_of(axis, bit):
    mine = my_bit(axis, bit)
    other = lax.axis_index(axis) + (1 - 2 * mine) * (1 << bit)
    if axis == "recv":
        return (other, lax.axis_index("send"))
    return (lax.axis_index("recv"), other)


def greet(moves):
    barrier = pltpu.get_barrier_semaphore()
    for axis, bit in moves:
        pl.semaphore_signal(barrier, inc=1, device_id=partner_of(axis, bit), device_id_type=MESH)
    pl.semaphore_wait(barrier, len(moves))


def run_streams(streams):
    live = list(streams)
    while live:
        after = []
        for stream in live:
            try:
                next(stream)
                after.append(stream)
            except StopIteration:
                pass
        live = after


def send_to(src, dst, sems, at, axis, bit):
    copy = pltpu.make_async_remote_copy(
        src_ref=src,
        dst_ref=dst,
        send_sem=sems.at[0, at],
        recv_sem=sems.at[1, at],
        device_id=partner_of(axis, bit),
        device_id_type=MESH,
    )
    copy.start()
    return copy


def gather_stream(table, sems, base, axis, order, cols):
    count = len(order)
    done = set()
    for at, bit in enumerate(order):
        index = []
        for dim in range(count):
            owner = count - 1 - dim
            index.append(pl.ds(0, 2) if owner in done else pl.ds(my_bit(axis, owner), 1))
        region = table.at[tuple(index) + (slice(None), cols)]
        copy = send_to(region, region, sems, base + at, axis, bit)
        yield
        copy.wait()
        done.add(bit)


def gather_kernel(plan, latent_ref, ts_ref, tr_ref, sems):
    for table, axis in ((ts_ref, "recv"), (tr_ref, "send")):
        count = table.ndim - 2
        at = tuple(my_bit(axis, count - 1 - dim) for dim in range(count))
        table[at] = latent_ref[...]
    greet(plan["moves"])
    streams = []
    base = 0
    for axis, order, cols in plan["gather"]:
        table = ts_ref if axis == "recv" else tr_ref
        streams.append(gather_stream(table, sems, base, axis, order, pl.ds(*cols)))
        base += len(order)
    run_streams(streams)


def add_rows(dst, left, right, rows):
    chunk = min(rows, 64)

    def body(i, carry):
        at = pl.ds(pl.multiple_of(i * chunk, chunk), chunk)
        dst[at, :] = left[at, :] + right[at, :]
        return carry

    lax.fori_loop(0, rows // chunk, body, 0)


def scatter_stream(source, slots, sems, base, axis, order, cols, out, width):
    held = source
    left = sorted(order, reverse=True)
    for at, bit in enumerate(order):
        place = left.index(bit)
        mine = my_bit(axis, bit)
        pick = lambda ref, which: ref.at[(slice(None),) * place + (which,)]
        if at == 0:
            outgoing = source.at[(slice(None),) * place + (1 - mine,) + (slice(None),) * (len(left) - place) + (cols,)]
            kept = source.at[(slice(None),) * place + (mine,) + (slice(None),) * (len(left) - place) + (cols,)]
        else:
            outgoing, kept = pick(held, 1 - mine), pick(held, mine)
        slot = slots[at]
        copy = send_to(outgoing, slot, sems, base + at, axis, bit)
        yield
        copy.wait()
        left.remove(bit)
        lead = 1 << len(left)
        for piece in range(lead):
            at_piece = tuple((piece >> (len(left) - 1 - d)) & 1 for d in range(len(left)))
            target = out.at[:, cols] if not left else slot.at[at_piece]
            first = slot.at[at_piece] if left else slot
            second = kept.at[at_piece] if left else kept
            add_rows(target, first, second, block_rows)
        held = slot


def total_stream(source, slots, sems, base, order, cols, out, factor):
    rows = source.shape[0]
    held, offset = source.at[:, cols], 0
    trail = []
    for at, (axis, bit) in enumerate(order):
        rows //= 2
        mine = my_bit(axis, bit)
        slot = slots[at]
        outgoing = held.at[pl.ds(pl.multiple_of((1 - mine) * rows, rows), rows)]
        kept = held.at[pl.ds(pl.multiple_of(mine * rows, rows), rows)]
        copy = send_to(outgoing, slot, sems, base + at, axis, bit)
        yield
        copy.wait()
        add_rows(slot, slot, kept, rows)
        held = slot
        offset = offset + mine * rows
        trail.append((axis, bit, rows, offset))
    out[pl.ds(pl.multiple_of(offset, rows), rows), cols] = held[...] * factor
    base += len(order)
    for at, (axis, bit, rows, offset) in enumerate(reversed(trail)):
        region = out.at[pl.ds(pl.multiple_of(offset, rows), rows), cols]
        copy = send_to(region, region, sems, base + at, axis, bit)
        yield
        copy.wait()


def small_stream(source, slots, sems, base, order, out, factor):
    out[...] = source[...]
    for at, (axis, bit) in enumerate(order):
        held = source if at == 0 else slots.at[2 * at - 1]
        copy = send_to(held, slots.at[2 * at], sems, base + at, axis, bit)
        yield
        copy.wait()
        slots[2 * at + 1] = held[...] + slots[2 * at]
    out[...] = slots[2 * len(order) - 1] * factor


def reduce_kernel(plan, factor, s_ref, r_ref, g_ref, small_ref, s_out, r_out, g_out, small_out, sems, small_slots, *slots):
    greet(plan["moves"])
    streams = []
    base = 0
    used = 0
    for axis, order, cols in plan["scatter"]:
        source, out = (s_ref, s_out) if axis == "recv" else (r_ref, r_out)
        streams.append(
            scatter_stream(source, slots[used : used + len(order)], sems, base, axis, order, pl.ds(*cols), out, cols[1])
        )
        base += len(order)
        used += len(order)
    for order, cols in plan["total"]:
        streams.append(
            total_stream(g_ref, slots[used : used + len(order)], sems, base, order, pl.ds(*cols), g_out, factor)
        )
        base += 2 * len(order)
        used += len(order)
    streams.append(small_stream(small_ref, small_slots, sems, base, plan["moves"], small_out, factor))
    run_streams(streams)


def edge_kernel(
    live_ref,
    edge_ref,
    cot_ref,
    scol_ref,
    srow_ref,
    rcol_ref,
    rrow_ref,
    ts_ref,
    tr_ref,
    w1_ref,
    b1_ref,
    w2_ref,
    b2_ref,
    gain_ref,
    edge_out,
    s_out,
    r_out,
    g_out,
    small_out,
    w1h,
    w1l,
    w2h,
    w2l,
    psh,
    psl,
    prh,
    prl,
):
    width = w2_ref.shape[0]
    send_nodes, recv_nodes = ts_ref.shape[0], tr_ref.shape[0]
    slots = edge_ref.shape[0]
    live_limit = block_rows * live_ref[0]

    def rows_at(i, rows=step_rows):
        return pl.ds(pl.multiple_of(i * rows, rows), rows)

    def split_first(i, carry):
        at = rows_at(i)
        w1h[at, :], w1l[at, :] = split(w1_ref[at, :])
        return carry

    def split_second(i, carry):
        at = rows_at(i)
        w2h[at, :], w2l[at, :] = split(w2_ref[at, :])
        return carry

    lax.fori_loop(0, 3 * width // step_rows, split_first, 0)
    lax.fori_loop(0, width // step_rows, split_second, 0)
    part = [pl.ds(k * width, width) for k in range(3)]

    def project(table, high, low, rows):
        def body(i, carry):
            at = rows_at(i)
            value = dot3(split(table[at, :]), (w1h[rows, :], w1l[rows, :]), NN)
            high[at, :], low[at, :] = split(value)
            return carry

        lax.fori_loop(0, table.shape[0] // step_rows, body, 0)

    project(ts_ref, psh, psl, part[1])
    project(tr_ref, prh, prl, part[2])
    s_out[...] = jnp.zeros_like(s_out)
    r_out[...] = jnp.zeros_like(r_out)
    g_out[...] = jnp.zeros_like(g_out)
    small_out[...] = jnp.zeros_like(small_out)

    def step(i, carry):
        at = rows_at(i)
        edge_rows = edge_ref[at, :]
        edge_parts = split(edge_rows)
        position = i * step_rows + lax.broadcasted_iota(jnp.int32, (step_rows, 1), 0)
        grad_rows = cot_ref[at, :] * (position < live_limit).astype(jnp.float32)

        def pick(col, nodes):
            lane = lax.broadcasted_iota(jnp.int32, (step_rows, nodes), 1)
            return (col[at, :] == lane).astype(jnp.float32).astype(jnp.bfloat16)

        def spread(row, nodes):
            line = lax.broadcasted_iota(jnp.int32, (nodes, step_rows), 0)
            return (row[:, at] == line).astype(jnp.float32).astype(jnp.bfloat16)

        hidden = dot3(edge_parts, (w1h[part[0], :], w1l[part[0], :]), NN)
        hidden = hidden + dot2(pick(scol_ref, send_nodes), (psh[...], psl[...]))
        hidden = hidden + dot2(pick(rcol_ref, recv_nodes), (prh[...], prl[...]))
        hidden = hidden + b1_ref[...]
        sigmoid_hidden = jax.nn.sigmoid(hidden)
        active = split(hidden * sigmoid_hidden)
        second = (w2h[...], w2l[...])
        output = dot3(active, second, NN) + b2_ref[...]
        centred = output - jnp.mean(output, axis=1, keepdims=True)
        inv_std = lax.rsqrt(jnp.mean(centred * centred, axis=1, keepdims=True) + norm_eps)
        normed = centred * inv_std
        scaled = grad_rows * gain_ref[...]
        norm_grad = inv_std * (
            scaled
            - jnp.mean(scaled, axis=1, keepdims=True)
            - normed * jnp.mean(scaled * normed, axis=1, keepdims=True)
        )
        norm_parts = split(norm_grad)
        hidden_grad = dot3(norm_parts, second, NT) * sigmoid_hidden * (1.0 + hidden * (1.0 - sigmoid_hidden))
        hidden_parts = split(hidden_grad)
        edge_out[at, :] = grad_rows + dot3(hidden_parts, (w1h[part[0], :], w1l[part[0], :]), NT)
        g_out[part[0], :] += dot3(edge_parts, hidden_parts, TN)
        g_out[pl.ds(3 * width, width), :] += dot3(active, norm_parts, TN)
        small_out[0:1, :] += jnp.sum(hidden_grad, axis=0, keepdims=True)
        small_out[1:2, :] += jnp.sum(norm_grad, axis=0, keepdims=True)
        small_out[2:3, :] += jnp.sum(grad_rows * normed, axis=0, keepdims=True)
        small_out[3:4, :] += jnp.sum(grad_rows, axis=0, keepdims=True)
        s_out[...] += dot2(spread(srow_ref, send_nodes), hidden_parts)
        r_out[...] += dot2(spread(rrow_ref, recv_nodes), hidden_parts)
        return carry

    steps = (live_limit + step_rows - 1) // step_rows
    lax.fori_loop(0, steps, step, 0)

    def blank(i, carry):
        edge_out[rows_at(i), :] = jnp.zeros((step_rows, width), jnp.float32)
        return carry

    lax.fori_loop(steps, slots // step_rows, blank, 0)

    def outer(table, sums, rows):
        def body(i, carry):
            at = rows_at(i)
            g_out[rows, :] += dot3(split(table[at, :]), split(sums[at, :]), TN)
            return carry

        lax.fori_loop(0, table.shape[0] // step_rows, body, 0)

    outer(ts_ref, s_out, part[1])
    outer(tr_ref, r_out, part[2])


def f32(*shape):
    return jax.ShapeDtypeStruct(shape, jnp.float32)


def make_plan(recv_bits, send_bits, width):
    half = width // 2
    recv_up = list(range(recv_bits))
    send_up = list(range(send_bits))
    recv_down, send_down = recv_up[::-1], send_up[::-1]
    recv_moves = [("recv", bit) for bit in recv_up]
    send_moves = [("send", bit) for bit in send_up]
    late_first = send_up[1:] + send_up[:1]
    return {
        "moves": recv_moves + send_moves,
        "gather": [
            ("recv", recv_down, (0, width)),
            ("send", send_down, (0, half)),
            ("send", send_up[:1] + send_down[:-1], (half, half)),
        ],
        "scatter": [
            ("recv", recv_up, (0, width)),
            ("send", send_up, (0, half)),
            ("send", late_first, (half, half)),
        ],
        "total": [
            (recv_moves + send_moves, (0, half)),
            (recv_moves[:1] + send_moves + recv_moves[1:], (half, half)),
        ],
    }


def shards(
    latent,
    edge_feat,
    senders,
    receivers,
    live_blocks,
    cotangent,
    w_first,
    first_bias,
    w_second,
    second_bias,
    norm_gain,
):
    node_rows, width = latent.shape
    slot_count = edge_feat.shape[0]
    recv_count = lax.axis_size("recv")
    send_count = lax.axis_size("send")
    recv_bits, send_bits = bits_of(recv_count), bits_of(send_count)
    recv_index = lax.axis_index("recv")
    recv_local = receivers - recv_index * (send_count * node_rows)
    send_local = senders // node_rows // send_count * node_rows + senders % node_rows
    plan = make_plan(recv_bits, send_bits, width)
    factor = 1.0 / math.sqrt(slot_count * recv_count * send_count)
    vmem = pl.BlockSpec(memory_space=pltpu.VMEM)
    recv_shape = (2,) * recv_bits + (node_rows, width)
    send_shape = (2,) * send_bits + (node_rows, width)

    copies = sum(len(order) for _, order, _ in plan["gather"])
    send_table, recv_table = pl.pallas_call(
        functools.partial(gather_kernel, plan),
        out_shape=(f32(*recv_shape), f32(*send_shape)),
        in_specs=[vmem],
        out_specs=(vmem, vmem),
        scratch_shapes=[pltpu.SemaphoreType.DMA((2, copies))],
        compiler_params=pltpu.CompilerParams(collective_id=0, has_side_effects=True, vmem_limit_bytes=40 << 20),
        name="gather_nodes",
    )(latent)
    send_table = send_table.reshape(recv_count * node_rows, width)
    recv_table = recv_table.reshape(send_count * node_rows, width)

    smem = pl.BlockSpec(memory_space=pltpu.SMEM)
    send_nodes, recv_nodes = send_table.shape[0], recv_table.shape[0]
    half_type = jnp.bfloat16
    edge_out, send_sum, recv_sum, weights, small = pl.pallas_call(
        edge_kernel,
        out_shape=(
            f32(slot_count, width),
            f32(send_nodes, width),
            f32(recv_nodes, width),
            f32(4 * width, width),
            f32(8, width),
        ),
        in_specs=[smem] + [vmem] * 13,
        out_specs=(vmem,) * 5,
        scratch_shapes=[
            pltpu.VMEM((3 * width, width), half_type),
            pltpu.VMEM((3 * width, width), half_type),
            pltpu.VMEM((width, width), half_type),
            pltpu.VMEM((width, width), half_type),
            pltpu.VMEM((send_nodes, width), half_type),
            pltpu.VMEM((send_nodes, width), half_type),
            pltpu.VMEM((recv_nodes, width), half_type),
            pltpu.VMEM((recv_nodes, width), half_type),
        ],
        compiler_params=pltpu.CompilerParams(vmem_limit_bytes=60 << 20),
        name="edge_work",
    )(
        live_blocks,
        edge_feat,
        cotangent,
        send_local[:, None],
        send_local[None, :],
        recv_local[:, None],
        recv_local[None, :],
        send_table,
        recv_table,
        w_first,
        first_bias[None, :],
        w_second,
        second_bias[None, :],
        norm_gain[None, :],
    )

    slots = []
    copies = 0
    for _, order, cols in plan["scatter"]:
        for at in range(len(order)):
            slots.append(pltpu.VMEM((2,) * (len(order) - 1 - at) + (node_rows, cols[1]), jnp.float32))
        copies += len(order)
    for order, cols in plan["total"]:
        for at in range(len(order)):
            slots.append(pltpu.VMEM((4 * width >> (at + 1), cols[1]), jnp.float32))
        copies += 2 * len(order)
    moves = len(plan["moves"])
    copies += moves
    send_own, recv_own, weight_total, small_total = pl.pallas_call(
        functools.partial(reduce_kernel, plan, factor),
        out_shape=(f32(node_rows, width), f32(node_rows, width), f32(4 * width, width), f32(8, width)),
        in_specs=[vmem] * 4,
        out_specs=(vmem,) * 4,
        scratch_shapes=[
            pltpu.SemaphoreType.DMA((2, copies)),
            pltpu.VMEM((2 * moves, 8, width), jnp.float32),
        ]
        + slots,
        compiler_params=pltpu.CompilerParams(collective_id=1, has_side_effects=True, vmem_limit_bytes=56 << 20),
        name="sum_grads",
    )(send_sum.reshape(recv_shape), recv_sum.reshape(send_shape), weights, small)

    def back(sums, rows):
        return lax.dot_general(
            sums, rows, NT, precision=lax.Precision.HIGHEST, preferred_element_type=jnp.float32
        )

    return (
        edge_out,
        back(send_own, w_first[width : 2 * width]),
        back(recv_own, w_first[2 * width :]),
        weight_total[: 3 * width],
        weight_total[3 * width :],
        small_total[:4],
    )


def solution(mesh):
    return jax.shard_map(
        shards,
        mesh=mesh,
        in_specs=(
            P(("recv", "send"), None),
            P(("recv", "send"), None),
            P(("recv", "send")),
            P(("recv", "send")),
            P(("recv", "send")),
            P(("recv", "send"), None),
            P(),
            P(),
            P(),
            P(),
            P(),
        ),
        out_specs=(
            P(("recv", "send"), None),
            P(("recv", "send"), None),
            P(("recv", "send"), None),
            P(),
            P(),
            P(),
        ),
        check_vma=False,
    )
```

time: 653 us -> 178 us (0.27)
  blocking collectives: 312 us -> 0 us
  waiting for transfers between devices: 266 us -> 0 us
  Pallas kernels: 0 us -> 158 us
  other arithmetic: 22.9 us -> 1.4 us
  between operations: 14.5 us -> 1.34 us
  matrix products: 17 us -> 5.81 us
    psum x1 -> x0, blocking collectives: 312 us -> none  [shards(): lax.psum((first_grad, second_grad, small_grads), ('recv', 'send'))]
    pallas_call x0 -> x3, Pallas kernels: none -> 158 us  [the longest x1 83.9 us: shards(): pl.pallas_call(functools.partial(reduce_kernel, plan, factor), out_shape=...]
    psum x1 -> x0, waiting for transfers between devices: 101 us -> none  [shards(): lax.psum((first_grad, second_grad, small_grads), ('recv', 'send'))]
    reduce_scatter x2 -> x0, waiting for transfers between devices: 92.7 us -> none  [the longest x1 72.1 us: shards(): lax.psum_scatter(receiver_acc, 'send', scatter_dimension=0, tiled=True)]
    all_gather x2 -> x0, waiting for transfers between devices: 70.4 us -> none  [the longest x1 51.5 us: shards(): receiver_table = lax.all_gather(latent, 'send', axis=0, tiled=True)]
    dot_general x6 -> x2, matrix products: 17 us -> 5.81 us  [back(): lax.dot_general(sums, rows, NT, precision=lax.Precision.HIGHEST, preferre...]
    scatter-add x2 -> x0, other arithmetic: 8.63 us -> none  [the longest x1 4.68 us: block_work(): receiver_acc.at[recv_ids].add(joined_grad[:, 2 * model_width:])]
    mul x3 -> x0, other arithmetic: 6.84 us -> none  [the longest x1 3.93 us: shards(): first_total * factor]
  transfers between devices with their start and end apart: 5 -> 0, of which waited for: 5 -> 0; matrix products, arithmetic and copies ran while one was open for 1% -> 0% of each run, Pallas kernels for 0% -> 0%
where the time goes in v1:
time: 178 us
  Pallas kernels  158 us (89%)
  local copies, waits for them, and re-layouts  10.9 us (6%)
  matrix products  5.81 us (3%)
    pallas_call x1, Pallas kernels, shards(): pl.pallas_call(functools.partial(reduce_kernel, plan, factor), out_shape=...  83.9 us
    pallas_call x1, Pallas kernels, shards(): pl.pallas_call(functools.partial(gather_kernel, plan), out_shape=(f32(*re...  38.1 us
    pallas_call x1, Pallas kernels, shards(): pl.pallas_call(edge_kernel, out_shape=(f32(slot_count, width), f32(send_n...  36 us
    dot_general x2, matrix products, back(): lax.dot_general(sums, rows, NT, precision=lax.Precision.HIGHEST, preferre...  5.81 us

profile of v1, /device:TPU:0, one launch (start us, length us, event | category | flops | bytes accessed | tf_op | source)
XLA Modules:
  0.0 177.5 jit_solution(12954237165250598597)
XLA Ops:
  1.3 0.7 broadcast_subtract_fusion
  2.0 0.0 copy-start.5
  2.0 0.7 fusion.6
  2.7 0.0 copy-start.6
  2.7 1.0 copy.17.scol_ref
  3.7 1.0 copy.18.rcol_ref
  4.8 0.0 copy-start.2
  4.8 0.9 copy-done.2
  5.7 38.1 %gather_nodes.1 = (f32[2,2,128,512]{3,2,1,0:T(8,128)S(1)}, f32[2,2,2,128,512]{4,3,2,1,0:T(8,128)S(1)}) custom-call(f32[128,512]{1,0:T(8,128)S(1)} %copy-done.2), custom_call_target="tpu_custom_call" | custom-call | tf_op jit(solution)/shard_map/gather_nodes/pallas_call | solution.py:407
  43.9 0.0 copy-start
  43.9 1.3 copy-done
  45.2 0.0 copy-start.1
  45.2 1.0 copy-done.1
  46.1 0.0 copy-done.5
  46.1 0.0 copy-done.6
  46.2 36.0 %edge_work.1 = (f32[1024,512]{1,0:T(8,128)}, f32[512,512]{1,0:T(8,128)}, f32[1024,512]{1,0:T(8,128)}, f32[2048,512]{1,0:T(8,128)}, f32[8,512]{1,0:T(8,128)}) custom-call(s32[1]{0:T(128)S(6)} %copy.19.live_ref, f32[1024,512]{1,0:T(8,128)} %edge_ref.1, f32[1024,512]{1,0:T(8,128)} %cot_ref.1, s32[1024,1]{1,0:T(8,128)} %copy.17.scol_ref, s32[1,1024]{1,0:T(1,128)} %bitcast.20, ...), custom_call_target="tpu_custom_call" | custom-call | tf_op jit(solution)/shard_map/edge_work/pallas_call | solution.py:422
  82.2 0.0 copy-start.3
  82.2 83.9 %sum_grads.1 = (f32[128,512]{1,0:T(8,128)}, f32[128,512]{1,0:T(8,128)}, f32[2048,512]{1,0:T(8,128)}, f32[8,512]{1,0:T(8,128)}) custom-call(f32[2,2,128,512]{3,2,1,0:T(8,128)} %bitcast.16, f32[2,2,2,128,512]{4,3,2,1,0:T(8,128)} %bitcast.15, f32[2048,512]{1,0:T(8,128)} %get-tuple-element.22.g_ref, f32[8,512]{1,0:T(8,128)} %get-tuple-element.23.small_ref), custom_call_target="tpu_custom_call" | custom-call | tf_op jit(solution)/shard_map/sum_grads/pallas_call | solution.py:474
  166.1 0.0 copy-start.4
  166.1 0.0 copy-done.3
  166.2 3.0 %fusion.2 = f32[128,512]{1,0:T(8,128)} fusion(f32[128,512]{1,0:T(8,128)} %get-tuple-element.24, f32[1536,512]{1,0:T(8,128)S(1)} %copy-done.3), kind=kOutput, calls=%fused_computation.2 | convolution fusion | flops 402653184 | bytes 1572864 | tf_op jit(solution)/shard_map/dot_general | solution.py:489
  169.1 2.8 %fusion = f32[128,512]{1,0:T(8,128)} fusion(f32[128,512]{1,0:T(8,128)} %get-tuple-element.25, f32[1536,512]{1,0:T(8,128)S(1)} %copy-done.3), kind=kOutput, calls=%fused_computation | convolution fusion | flops 402653184 | bytes 1572864 | tf_op jit(solution)/shard_map/dot_general | solution.py:489
  172.0 1.3 slice.19
  173.3 2.3 %slice.18 = f32[512,512]{1,0:T(8,128)} slice(f32[2048,512]{1,0:T(8,128)} %get-tuple-element.26), slice={[1536:2048], [0:512]} | slice | bytes 2097152 | tf_op jit(solution)/shard_map/slice | solution.py:498
  175.5 0.0 copy-done.4
  175.5 2.0 %slice.17 = f32[1536,512]{1,0:T(8,128)} slice(f32[2048,512]{1,0:T(8,128)S(1)} %copy-done.4), slice={[0:1536], [0:512]} | slice | bytes 6291456 | tf_op jit(solution)/shard_map/slice | solution.py:497
Async XLA Ops:
  2.0 44.2 %copy-start.5 = (s32[1024]{0:T(1024)}, s32[1024]{0:T(1024)S(1)}, u32[]{:S(2)}) copy-start(s32[1024]{0:T(1024)S(1)} %broadcast_subtract_fusion) | copy-start | bytes 12292
  2.7 43.5 %copy-start.6 = (s32[1024]{0:T(1024)}, s32[1024]{0:T(1024)S(1)}, u32[]{:S(2)}) copy-start(s32[1024]{0:T(1024)S(1)} %fusion.6) | copy-start | bytes 12292
  4.8 0.9 copy-start.2
  43.9 1.3 copy-start
  45.2 1.0 copy-start.1
  82.2 84.0 %copy-start.3 = (f32[1536,512]{1,0:T(8,128)S(1)}, f32[1536,512]{1,0:T(8,128)}, u32[]{:S(2)}) copy-start(f32[1536,512]{1,0:T(8,128)} %w1_ref.1) | copy-start | bytes 9437188
  166.1 9.4 %copy-start.4 = (f32[2048,512]{1,0:T(8,128)S(1)}, f32[2048,512]{1,0:T(8,128)}, u32[]{:S(2)}) copy-start(f32[2048,512]{1,0:T(8,128)} %get-tuple-element.26) | copy-start | bytes 12582916

commit v2 on v1

v2 whole, which is shorter than its diff:
```python
import functools
import math

import jax
import jax.numpy as jnp
from jax import lax
from jax.experimental import pallas as pl
from jax.experimental.pallas import tpu as pltpu
from jax.sharding import PartitionSpec as P

norm_eps = 1e-05
block_rows = 128
step_rows = 256
MESH = pl.DeviceIdType.MESH
NN = (((1,), (0,)), ((), ()))
NT = (((1,), (1,)), ((), ()))
TN = (((0,), (0,)), ((), ()))


def split(value):
    high = value.astype(jnp.bfloat16)
    low = (value - high.astype(jnp.float32)).astype(jnp.bfloat16)
    return high, low


def mm(left, right, dims):
    return lax.dot_general(left, right, dims, preferred_element_type=jnp.float32)


def dot3(left, right, dims):
    return mm(left[0], right[0], dims) + mm(left[0], right[1], dims) + mm(left[1], right[0], dims)


def dot2(exact, right):
    return mm(exact, right[0], NN) + mm(exact, right[1], NN)


def bits_of(count):
    return max(count.bit_length() - 1, 0)


def my_bit(axis, bit):
    return (lax.axis_index(axis) // (1 << bit)) % 2


def partner_of(axis, bit):
    mine = my_bit(axis, bit)
    other = lax.axis_index(axis) + (1 - 2 * mine) * (1 << bit)
    if axis == "recv":
        return (other, lax.axis_index("send"))
    return (lax.axis_index("recv"), other)


def greet(moves):
    barrier = pltpu.get_barrier_semaphore()
    for axis, bit in moves:
        pl.semaphore_signal(barrier, inc=1, device_id=partner_of(axis, bit), device_id_type=MESH)
    pl.semaphore_wait(barrier, len(moves))


def run_streams(streams):
    live = list(streams)
    while live:
        after = []
        for stream in live:
            try:
                next(stream)
                after.append(stream)
            except StopIteration:
                pass
        live = after


def send_to(src, dst, sems, at, axis, bit):
    copy = pltpu.make_async_remote_copy(
        src_ref=src,
        dst_ref=dst,
        send_sem=sems.at[0, at],
        recv_sem=sems.at[1, at],
        device_id=partner_of(axis, bit),
        device_id_type=MESH,
    )
    copy.start()
    return copy


def gather_stream(table, sems, base, axis, order, cols):
    count = len(order)
    done = set()
    for at, bit in enumerate(order):
        index = []
        for dim in range(count):
            owner = count - 1 - dim
            index.append(pl.ds(0, 2) if owner in done else pl.ds(my_bit(axis, owner), 1))
        region = table.at[tuple(index) + (slice(None), cols)]
        copy = send_to(region, region, sems, base + at, axis, bit)
        yield
        copy.wait()
        done.add(bit)


def add_rows(dst, left, right, rows):
    chunk = min(rows, 64)

    def body(i, carry):
        at = pl.ds(pl.multiple_of(i * chunk, chunk), chunk)
        dst[at, :] = left[at, :] + right[at, :]
        return carry

    lax.fori_loop(0, rows // chunk, body, 0)


def scatter_stream(source, slots, sems, base, axis, order, cols, out, width):
    held = source
    left = sorted(order, reverse=True)
    for at, bit in enumerate(order):
        place = left.index(bit)
        mine = my_bit(axis, bit)
        pick = lambda ref, which: ref.at[(slice(None),) * place + (which,)]
        if at == 0:
            outgoing = source.at[(slice(None),) * place + (1 - mine,) + (slice(None),) * (len(left) - place) + (cols,)]
            kept = source.at[(slice(None),) * place + (mine,) + (slice(None),) * (len(left) - place) + (cols,)]
        else:
            outgoing, kept = pick(held, 1 - mine), pick(held, mine)
        slot = slots[at]
        copy = send_to(outgoing, slot, sems, base + at, axis, bit)
        yield
        copy.wait()
        left.remove(bit)
        lead = 1 << len(left)
        for piece in range(lead):
            at_piece = tuple((piece >> (len(left) - 1 - d)) & 1 for d in range(len(left)))
            target = out.at[:, cols] if not left else slot.at[at_piece]
            first = slot.at[at_piece] if left else slot
            second = kept.at[at_piece] if left else kept
            add_rows(target, first, second, block_rows)
        held = slot


def total_stream(source, slots, sems, base, order, start, rows, cols, out, factor):
    held, offset = source.at[pl.ds(start, rows), cols], 0
    trail = []
    for at, (axis, bit) in enumerate(order):
        slot = slots[at]
        if rows > 8:
            rows //= 2
            mine = my_bit(axis, bit)
            outgoing = held.at[pl.ds(pl.multiple_of((1 - mine) * rows, rows), rows)]
            kept = held.at[pl.ds(pl.multiple_of(mine * rows, rows), rows)]
            offset = offset + mine * rows
            trail.append((axis, bit, rows, offset))
        else:
            outgoing = kept = held
        copy = send_to(outgoing, slot, sems, base + at, axis, bit)
        yield
        copy.wait()
        add_rows(slot, slot, kept, rows)
        held = slot
    out[pl.ds(pl.multiple_of(start + offset, 8), rows), cols] = held[...] * factor
    base += len(order)
    for at, (axis, bit, rows, offset) in enumerate(reversed(trail)):
        region = out.at[pl.ds(pl.multiple_of(start + offset, 8), rows), cols]
        copy = send_to(region, region, sems, base + at, axis, bit)
        yield
        copy.wait()


def small_stream(source, slots, sems, base, order, out, factor):
    out[...] = source[...]
    for at, (axis, bit) in enumerate(order):
        held = source if at == 0 else slots.at[2 * at - 1]
        copy = send_to(held, slots.at[2 * at], sems, base + at, axis, bit)
        yield
        copy.wait()
        slots[2 * at + 1] = held[...] + slots[2 * at]
    out[...] = slots[2 * len(order) - 1] * factor


def rows_at(i, rows=step_rows):
    return pl.ds(pl.multiple_of(i * rows, rows), rows)


def loop(count, body):
    def run(i, carry):
        body(i)
        return carry

    lax.fori_loop(0, count, run, 0)


def whole_kernel(
    plan,
    factor,
    live_ref,
    latent_ref,
    edge_hbm,
    cot_hbm,
    scol_ref,
    srow_ref,
    rcol_ref,
    rrow_ref,
    w1_hbm,
    b1_ref,
    w2_hbm,
    b2_ref,
    gain_ref,
    edge_out,
    s_own,
    r_own,
    g_out,
    small_out,
    sems,
    local_sems,
    edge_ref,
    cot_ref,
    wh,
    wl,
    ts_ref,
    tr_ref,
    ps_ref,
    pr_ref,
    g_ref,
    small_ref,
    own_s,
    own_r,
    small_slots,
    *slots,
):
    slot_count, width = edge_ref.shape
    steps = slot_count // step_rows
    live_limit = block_rows * live_ref[0]
    part = [pl.ds(k * width, width) for k in range(4)]
    node_rows = latent_ref.shape[0]
    send_pieces = [tuple((k >> (ts_ref.ndim - 3 - d)) & 1 for d in range(ts_ref.ndim - 2)) for k in range(1 << (ts_ref.ndim - 2))]
    recv_pieces = [tuple((k >> (tr_ref.ndim - 3 - d)) & 1 for d in range(tr_ref.ndim - 2)) for k in range(1 << (tr_ref.ndim - 2))]

    loads = [
        pltpu.make_async_copy(w2_hbm, g_out.at[part[0]], local_sems.at[0]),
        pltpu.make_async_copy(w1_hbm, g_out.at[pl.ds(width, 3 * width)], local_sems.at[1]),
        pltpu.make_async_copy(edge_hbm, edge_ref, local_sems.at[2]),
        pltpu.make_async_copy(cot_hbm, cot_ref, local_sems.at[3]),
    ]
    for load in loads:
        load.start()
    for table, axis in ((ts_ref, "recv"), (tr_ref, "send")):
        count = table.ndim - 2
        at = tuple(my_bit(axis, count - 1 - dim) for dim in range(count))
        table[at] = latent_ref[...]
    greet(plan["moves"])

    streams = []
    base = 0
    for axis, order, cols in plan["gather"]:
        table = ts_ref if axis == "recv" else tr_ref
        streams.append(gather_stream(table, sems, base, axis, order, pl.ds(*cols)))
        base += len(order)

    def prepare():
        yield
        for load in loads:
            load.wait()

        def split_rows(i):
            at = rows_at(i)
            wh[at, :], wl[at, :] = split(g_out[at, :])

        loop(4 * width // step_rows, split_rows)

        def first_part(i):
            at = rows_at(i)
            edge_out[at, :] = dot3(split(edge_ref[at, :]), (wh[part[1], :], wl[part[1], :]), NN) + b1_ref[...]

        loop(steps, first_part)
        yield

    def project(table, pieces, into, rows):
        for k, piece in enumerate(pieces):
            into[piece] = dot3(split(table[piece]), (wh[rows, :], wl[rows, :]), NN)

    run_streams(streams + [prepare()])
    project(ts_ref, send_pieces, ps_ref, part[2])
    project(tr_ref, recv_pieces, pr_ref, part[3])

    small_ref[...] = jnp.zeros_like(small_ref)
    g_ref[part[0], :] = jnp.zeros((width, width), jnp.float32)
    send_nodes, recv_nodes = len(send_pieces) * node_rows, len(recv_pieces) * node_rows

    def step(i):
        at = rows_at(i)
        position = i * step_rows + lax.broadcasted_iota(jnp.int32, (step_rows, 1), 0)
        grad_rows = cot_ref[at, :] * (position < live_limit).astype(jnp.float32)
        cot_ref[at, :] = grad_rows

        def pick(col, nodes):
            lane = lax.broadcasted_iota(jnp.int32, (step_rows, nodes), 1)
            return (col[at, :] == lane).astype(jnp.float32).astype(jnp.bfloat16)

        send_table = split(ps_ref[...].reshape(send_nodes, width))
        recv_table = split(pr_ref[...].reshape(recv_nodes, width))
        hidden = edge_out[at, :] + dot2(pick(scol_ref, send_nodes), send_table)
        hidden = hidden + dot2(pick(rcol_ref, recv_nodes), recv_table)
        sigmoid_hidden = jax.nn.sigmoid(hidden)
        active = split(hidden * sigmoid_hidden)
        second = (wh[part[0], :], wl[part[0], :])
        output = dot3(active, second, NN) + b2_ref[...]
        centred = output - jnp.mean(output, axis=1, keepdims=True)
        inv_std = lax.rsqrt(jnp.mean(centred * centred, axis=1, keepdims=True) + norm_eps)
        normed = centred * inv_std
        scaled = grad_rows * gain_ref[...]
        norm_grad = inv_std * (
            scaled
            - jnp.mean(scaled, axis=1, keepdims=True)
            - normed * jnp.mean(scaled * normed, axis=1, keepdims=True)
        )
        norm_parts = split(norm_grad)
        hidden_grad = dot3(norm_parts, second, NT) * sigmoid_hidden * (1.0 + hidden * (1.0 - sigmoid_hidden))
        edge_out[at, :] = hidden_grad
        g_ref[part[0], :] += dot3(active, norm_parts, TN)
        small_ref[0:1, :] += jnp.sum(hidden_grad, axis=0, keepdims=True)
        small_ref[1:2, :] += jnp.sum(norm_grad, axis=0, keepdims=True)
        small_ref[2:3, :] += jnp.sum(grad_rows * normed, axis=0, keepdims=True)
        small_ref[3:4, :] += jnp.sum(grad_rows, axis=0, keepdims=True)

    loop(steps, step)

    def spread_sums(row, pieces, into):
        hidden_parts = split(edge_out[...])
        for k, piece in enumerate(pieces):
            line = k * node_rows + lax.broadcasted_iota(jnp.int32, (node_rows, slot_count), 0)
            into[piece] = dot2((row[...] == line).astype(jnp.float32).astype(jnp.bfloat16), hidden_parts)

    def outer(table, pieces, sums, rows):
        g_ref[rows, :] = jnp.zeros((width, width), jnp.float32)
        for piece in pieces:
            g_ref[rows, :] += dot3(split(table[piece]), split(sums[piece]), TN)

    used = 0
    scatters = []
    for axis, order, cols in plan["scatter"]:
        source, out = (ps_ref, own_s) if axis == "recv" else (pr_ref, own_r)
        scatters.append(
            scatter_stream(source, slots[used : used + len(order)], sems, base, axis, order, pl.ds(*cols), out, cols[1])
        )
        base += len(order)
        used += len(order)
    totals = []
    for order, cols, start in plan["total"]:
        totals.append(
            total_stream(
                g_ref, slots[used : used + len(order)], sems, base, order, start, 2 * width, pl.ds(*cols), g_out, factor
            )
        )
        base += 2 * len(order)
        used += len(order)
    early = [t for t, (_, _, start) in zip(totals, plan["total"]) if start == 0]
    late = [t for t, (_, _, start) in zip(totals, plan["total"]) if start != 0]

    spread_sums(rrow_ref, recv_pieces, pr_ref)
    for stream in scatters[1:]:
        next(stream)
    spread_sums(srow_ref, send_pieces, ps_ref)
    next(scatters[0])

    def edge_outer(i):
        at = rows_at(i)
        g_ref[part[1], :] += dot3(split(edge_ref[at, :]), split(edge_out[at, :]), TN)

    g_ref[part[1], :] = jnp.zeros((width, width), jnp.float32)
    loop(steps, edge_outer)
    small = small_stream(small_ref, small_slots, sems, base, plan["moves"], small_out, factor)
    for stream in early:
        next(stream)
    next(small)
    outer(ts_ref, send_pieces, ps_ref, part[2])
    outer(tr_ref, recv_pieces, pr_ref, part[3])
    for stream in late:
        next(stream)

    def finish():
        yield

        def edge_back(i):
            at = rows_at(i)
            edge_out[at, :] = cot_ref[at, :] + dot3(split(edge_out[at, :]), (wh[part[1], :], wl[part[1], :]), NT)

        loop(steps, edge_back)
        for _ in range(6):
            yield

    run_streams(scatters + early + late + [small, finish()])
    s_own[...] = dot3(split(own_s[...]), (wh[part[2], :], wl[part[2], :]), NT)
    r_own[...] = dot3(split(own_r[...]), (wh[part[3], :], wl[part[3], :]), NT)


def f32(*shape):
    return jax.ShapeDtypeStruct(shape, jnp.float32)


def make_plan(recv_bits, send_bits, width):
    half = width // 2
    recv_up = list(range(recv_bits))
    send_up = list(range(send_bits))
    recv_down, send_down = recv_up[::-1], send_up[::-1]
    recv_moves = [("recv", bit) for bit in recv_up]
    send_moves = [("send", bit) for bit in send_up]
    late_first = send_up[1:] + send_up[:1]
    return {
        "moves": recv_moves + send_moves,
        "gather": [
            ("recv", recv_down, (0, width)),
            ("send", send_down, (0, half)),
            ("send", send_up[:1] + send_down[:-1], (half, half)),
        ],
        "scatter": [
            ("recv", recv_up, (0, width)),
            ("send", send_up, (0, half)),
            ("send", late_first, (half, half)),
        ],
        "total": [
            (recv_moves + send_moves, (0, half), 0),
            (recv_moves[:1] + send_moves + recv_moves[1:], (half, half), 0),
            (recv_moves + send_moves, (0, half), 2 * width),
            (recv_moves[:1] + send_moves + recv_moves[1:], (half, half), 2 * width),
        ],
    }


def shards(
    latent,
    edge_feat,
    senders,
    receivers,
    live_blocks,
    cotangent,
    w_first,
    first_bias,
    w_second,
    second_bias,
    norm_gain,
):
    node_rows, width = latent.shape
    slot_count = edge_feat.shape[0]
    recv_count = lax.axis_size("recv")
    send_count = lax.axis_size("send")
    recv_bits, send_bits = bits_of(recv_count), bits_of(send_count)
    recv_index = lax.axis_index("recv")
    recv_local = receivers - recv_index * (send_count * node_rows)
    send_local = senders // node_rows // send_count * node_rows + senders % node_rows
    plan = make_plan(recv_bits, send_bits, width)
    factor = 1.0 / math.sqrt(slot_count * recv_count * send_count)
    vmem = pl.BlockSpec(memory_space=pltpu.VMEM)
    recv_shape = (2,) * recv_bits + (node_rows, width)
    send_shape = (2,) * send_bits + (node_rows, width)

    anywhere = pl.BlockSpec(memory_space=pl.ANY)
    smem = pl.BlockSpec(memory_space=pltpu.SMEM)
    half_type = jnp.bfloat16
    slots = []
    copies = sum(len(order) for _, order, _ in plan["gather"])
    for _, order, cols in plan["scatter"]:
        for at in range(len(order)):
            slots.append(pltpu.VMEM((2,) * (len(order) - 1 - at) + (node_rows, cols[1]), jnp.float32))
        copies += len(order)
    for order, cols, start in plan["total"]:
        for at in range(len(order)):
            slots.append(pltpu.VMEM((max(2 * width >> (at + 1), 8), cols[1]), jnp.float32))
        copies += 2 * len(order)
    moves = len(plan["moves"])
    copies += moves
    edge_out, send_grad, recv_grad, weights, small = pl.pallas_call(
        functools.partial(whole_kernel, plan, factor),
        out_shape=(
            f32(slot_count, width),
            f32(node_rows, width),
            f32(node_rows, width),
            f32(4 * width, width),
            f32(8, width),
        ),
        in_specs=[smem, vmem, anywhere, anywhere, vmem, vmem, vmem, vmem, anywhere, vmem, anywhere, vmem, vmem],
        out_specs=(vmem,) * 5,
        scratch_shapes=[
            pltpu.SemaphoreType.DMA((2, copies)),
            pltpu.SemaphoreType.DMA((4,)),
            pltpu.VMEM((slot_count, width), jnp.float32),
            pltpu.VMEM((slot_count, width), jnp.float32),
            pltpu.VMEM((4 * width, width), half_type),
            pltpu.VMEM((4 * width, width), half_type),
            pltpu.VMEM(recv_shape, jnp.float32),
            pltpu.VMEM(send_shape, jnp.float32),
            pltpu.VMEM(recv_shape, jnp.float32),
            pltpu.VMEM(send_shape, jnp.float32),
            pltpu.VMEM((4 * width, width), jnp.float32),
            pltpu.VMEM((8, width), jnp.float32),
            pltpu.VMEM((node_rows, width), jnp.float32),
            pltpu.VMEM((node_rows, width), jnp.float32),
            pltpu.VMEM((2 * moves, 8, width), jnp.float32),
        ]
        + slots,
        compiler_params=pltpu.CompilerParams(collective_id=0, has_side_effects=True, vmem_limit_bytes=60 << 20),
        name="edge_block",
    )(
        live_blocks,
        latent,
        edge_feat,
        cotangent,
        send_local[:, None],
        send_local[None, :],
        recv_local[:, None],
        recv_local[None, :],
        w_first,
        first_bias[None, :],
        w_second,
        second_bias[None, :],
        norm_gain[None, :],
    )
    return (edge_out, send_grad, recv_grad, weights[width:], weights[:width], small[:4])


def solution(mesh):
    return jax.shard_map(
        shards,
        mesh=mesh,
        in_specs=(
            P(("recv", "send"), None),
            P(("recv", "send"), None),
            P(("recv", "send")),
            P(("recv", "send")),
            P(("recv", "send")),
            P(("recv", "send"), None),
            P(),
            P(),
            P(),
            P(),
            P(),
        ),
        out_specs=(
            P(("recv", "send"), None),
            P(("recv", "send"), None),
            P(("recv", "send"), None),
            P(),
            P(),
            P(),
        ),
        check_vma=False,
    )
```

time: 178 us -> 146 us (0.82)
  Pallas kernels: 158 us -> 130 us
  matrix products: 5.81 us -> 0 us
    pallas_call x3 -> x1, Pallas kernels: 158 us -> 130 us  [shards(): pl.pallas_call(functools.partial(whole_kernel, plan, factor), out_shape=(...]
    dot_general x2 -> x0, matrix products: 5.81 us -> none  [back(): lax.dot_general(sums, rows, NT, precision=lax.Precision.HIGHEST, preferre...]
    slice x3, local copies, waits for them, and re-layouts: 5.55 us -> 7.59 us  [the longest x1 4.01 us: shards(): weights[width:]]
where the time goes in v2:
time: 146 us; the launch traced here: 145 us
  Pallas kernels  130 us (89%)
  local copies, waits for them, and re-layouts  12.4 us (8%)
    pallas_call x1, Pallas kernels, shards(): pl.pallas_call(functools.partial(whole_kernel, plan, factor), out_shape=(...  130 us
    slice x1, local copies, waits for them, and re-layouts, shards(): weights[width:]  4.01 us

profile of v2, /device:TPU:0, one launch (start us, length us, event | category | flops | bytes accessed | tf_op | source)
XLA Modules:
  0.0 145.5 jit_solution(16469683938005955355)
XLA Ops:
  1.3 0.7 broadcast_subtract_fusion
  2.0 0.0 copy-start.3
  2.0 0.7 fusion.2
  2.7 0.0 copy-start.4
  2.7 1.0 copy.17.scol_ref
  3.7 1.0 copy.18.rcol_ref
  4.7 0.0 copy-done.3
  4.8 0.0 copy-done.4
  4.8 130.4 %edge_block.1 = (f32[1024,512]{1,0:T(8,128)}, f32[128,512]{1,0:T(8,128)}, f32[128,512]{1,0:T(8,128)}, f32[2048,512]{1,0:T(8,128)}, f32[8,512]{1,0:T(8,128)}) custom-call(s32[1]{0:T(128)S(6)} %copy.22.live_ref, f32[128,512]{1,0:T(8,128)} %latent_ref.1, f32[1024,512]{1,0:T(8,128)} %edge_hbm.1, f32[1024,512]{1,0:T(8,128)} %cot_hbm.1, s32[1024,1]{1,0:T(8,128)} %copy.17.scol_ref, ...), custom_call_target="tpu_custom_call" | custom-call | tf_op jit(solution)/shard_map/edge_block/pallas_call | solution.py:470
  135.1 1.3 slice.11
  136.5 2.3 %slice.10 = f32[512,512]{1,0:T(8,128)} slice(f32[2048,512]{1,0:T(8,128)} %get-tuple-element.14), slice={[0:512], [0:512]} | slice | bytes 2097152 | tf_op jit(solution)/shard_map/slice | solution.py:516
  138.7 0.0 copy-start
  138.7 4.0 %slice.9 = f32[1536,512]{1,0:T(8,128)} slice(f32[2048,512]{1,0:T(8,128)} %get-tuple-element.14), slice={[512:2048], [0:512]} | slice | bytes 6291456 | tf_op jit(solution)/shard_map/slice | solution.py:516
  142.7 0.0 copy-done
  142.7 0.0 copy-start.2
  142.7 0.0 copy-start.1
  142.7 1.3 copy.23
  144.1 0.0 copy-done.2
  144.1 0.7 copy.24
  144.8 0.0 copy-done.1
  144.8 0.7 copy.25
Async XLA Ops:
  2.0 2.8 %copy-start.3 = (s32[1024]{0:T(1024)}, s32[1024]{0:T(1024)S(1)}, u32[]{:S(2)}) copy-start(s32[1024]{0:T(1024)S(1)} %broadcast_subtract_fusion) | copy-start | bytes 12292
  2.7 2.1 %copy-start.4 = (s32[1024]{0:T(1024)}, s32[1024]{0:T(1024)S(1)}, u32[]{:S(2)}) copy-start(s32[1024]{0:T(1024)S(1)} %fusion.2) | copy-start | bytes 12292
  138.7 4.0 %copy-start = (f32[1024,512]{1,0:T(8,128)S(1)}, f32[1024,512]{1,0:T(8,128)}, u32[]{:S(2)}) copy-start(f32[1024,512]{1,0:T(8,128)} %get-tuple-element.22) | copy-start | bytes 6291460
  142.7 1.3 copy-start.2
  142.7 2.0 %copy-start.1 = (f32[128,512]{1,0:T(8,128)S(1)}, f32[128,512]{1,0:T(8,128)}, u32[]{:S(2)}) copy-start(f32[128,512]{1,0:T(8,128)} %get-tuple-element.24) | copy-start | bytes 786436

commit v3 on v2

--- a/solution.py
+++ b/solution.py
@@ -166,14 +166,13 @@
 
 
 def small_stream(source, slots, sems, base, order, out, factor):
-    out[...] = source[...]
     for at, (axis, bit) in enumerate(order):
         held = source if at == 0 else slots.at[2 * at - 1]
         copy = send_to(held, slots.at[2 * at], sems, base + at, axis, bit)
         yield
         copy.wait()
         slots[2 * at + 1] = held[...] + slots[2 * at]
-    out[...] = slots[2 * len(order) - 1] * factor
+    out[...] = slots[2 * len(order) - 1, : out.shape[0], :] * factor
 
 
 def rows_at(i, rows=step_rows):
@@ -195,22 +194,25 @@
     latent_ref,
     edge_hbm,
     cot_hbm,
-    scol_ref,
     srow_ref,
-    rcol_ref,
     rrow_ref,
     w1_hbm,
     b1_ref,
     w2_hbm,
     b2_ref,
     gain_ref,
-    edge_out,
+    edge_hbm_out,
     s_own,
     r_own,
-    g_out,
+    w1_hbm_out,
+    w2_hbm_out,
     small_out,
     sems,
     local_sems,
+    edge_out,
+    g_out,
+    scol_ref,
+    rcol_ref,
     edge_ref,
     cot_ref,
     wh,
@@ -255,7 +257,16 @@
         streams.append(gather_stream(table, sems, base, axis, order, pl.ds(*cols)))
         base += len(order)
 
+    send_stride = lax.axis_size("send") * node_rows
+    send_first = lax.axis_index("send") * node_rows
+    recv_first = lax.axis_index("recv") * send_stride
+    node_shift = node_rows.bit_length() - 1
+
     def prepare():
+        for k in range(slot_count // 128):
+            at = pl.ds(k * 128, 128)
+            scol_ref[at, :] = jnp.broadcast_to(srow_ref[:, at], (128, 128)).T - send_first
+            rcol_ref[at, :] = jnp.broadcast_to(rrow_ref[:, at], (128, 128)).T - recv_first
         yield
         for load in loads:
             load.wait()
@@ -272,13 +283,13 @@
 
         loop(steps, first_part)
         yield
+        project(ts_ref, send_pieces, ps_ref, part[2])
 
     def project(table, pieces, into, rows):
         for k, piece in enumerate(pieces):
             into[piece] = dot3(split(table[piece]), (wh[rows, :], wl[rows, :]), NN)
 
     run_streams(streams + [prepare()])
-    project(ts_ref, send_pieces, ps_ref, part[2])
     project(tr_ref, recv_pieces, pr_ref, part[3])
 
     small_ref[...] = jnp.zeros_like(small_ref)
@@ -291,14 +302,15 @@
         grad_rows = cot_ref[at, :] * (position < live_limit).astype(jnp.float32)
         cot_ref[at, :] = grad_rows
 
-        def pick(col, nodes):
-            lane = lax.broadcasted_iota(jnp.int32, (step_rows, nodes), 1)
-            return (col[at, :] == lane).astype(jnp.float32).astype(jnp.bfloat16)
+        def pick(col, nodes, gap):
+            lane = lax.broadcasted_iota(jnp.int32, (1, nodes), 1)
+            lane = lane + lax.shift_right_arithmetic(lane, jnp.int32(node_shift)) * gap
+            return (col[at, 0:1] == lane).astype(jnp.float32).astype(jnp.bfloat16)
 
         send_table = split(ps_ref[...].reshape(send_nodes, width))
         recv_table = split(pr_ref[...].reshape(recv_nodes, width))
-        hidden = edge_out[at, :] + dot2(pick(scol_ref, send_nodes), send_table)
-        hidden = hidden + dot2(pick(rcol_ref, recv_nodes), recv_table)
+        hidden = edge_out[at, :] + dot2(pick(scol_ref, send_nodes, send_stride - node_rows), send_table)
+        hidden = hidden + dot2(pick(rcol_ref, recv_nodes, 0), recv_table)
         sigmoid_hidden = jax.nn.sigmoid(hidden)
         active = split(hidden * sigmoid_hidden)
         second = (wh[part[0], :], wl[part[0], :])
@@ -323,10 +335,10 @@
 
     loop(steps, step)
 
-    def spread_sums(row, pieces, into):
+    def spread_sums(row, pieces, into, first, stride):
         hidden_parts = split(edge_out[...])
         for k, piece in enumerate(pieces):
-            line = k * node_rows + lax.broadcasted_iota(jnp.int32, (node_rows, slot_count), 0)
+            line = first + k * stride + lax.broadcasted_iota(jnp.int32, (node_rows, slot_count), 0)
             into[piece] = dot2((row[...] == line).astype(jnp.float32).astype(jnp.bfloat16), hidden_parts)
 
     def outer(table, pieces, sums, rows):
@@ -355,10 +367,10 @@
     early = [t for t, (_, _, start) in zip(totals, plan["total"]) if start == 0]
     late = [t for t, (_, _, start) in zip(totals, plan["total"]) if start != 0]
 
-    spread_sums(rrow_ref, recv_pieces, pr_ref)
+    spread_sums(rrow_ref, recv_pieces, pr_ref, recv_first, node_rows)
     for stream in scatters[1:]:
         next(stream)
-    spread_sums(srow_ref, send_pieces, ps_ref)
+    spread_sums(srow_ref, send_pieces, ps_ref, send_first, send_stride)
     next(scatters[0])
 
     def edge_outer(i):
@@ -376,20 +388,28 @@
     for stream in late:
         next(stream)
 
+    edge_store = pltpu.make_async_copy(edge_out, edge_hbm_out, local_sems.at[2])
+
     def finish():
-        yield
-
         def edge_back(i):
             at = rows_at(i)
             edge_out[at, :] = cot_ref[at, :] + dot3(split(edge_out[at, :]), (wh[part[1], :], wl[part[1], :]), NT)
 
         loop(steps, edge_back)
-        for _ in range(6):
-            yield
-
-    run_streams(scatters + early + late + [small, finish()])
+        edge_store.start()
+        yield
+
+    run_streams(early + late + [small, finish()] + scatters)
+    stores = [
+        pltpu.make_async_copy(g_out.at[part[0]], w2_hbm_out, local_sems.at[0]),
+        pltpu.make_async_copy(g_out.at[pl.ds(width, 3 * width)], w1_hbm_out, local_sems.at[1]),
+    ]
+    for store in stores:
+        store.start()
     s_own[...] = dot3(split(own_s[...]), (wh[part[2], :], wl[part[2], :]), NT)
     r_own[...] = dot3(split(own_r[...]), (wh[part[3], :], wl[part[3], :]), NT)
+    for store in stores + [edge_store]:
+        store.wait()
 
 
 def f32(*shape):
@@ -398,6 +418,7 @@
 
 def make_plan(recv_bits, send_bits, width):
     half = width // 2
+    most = width // 4 * 3
     recv_up = list(range(recv_bits))
     send_up = list(range(send_bits))
     recv_down, send_down = recv_up[::-1], send_up[::-1]
@@ -408,17 +429,17 @@
         "moves": recv_moves + send_moves,
         "gather": [
             ("recv", recv_down, (0, width)),
-            ("send", send_down, (0, half)),
-            ("send", send_up[:1] + send_down[:-1], (half, half)),
+            ("send", send_down, (0, most)),
+            ("send", send_up[:1] + send_down[:-1], (most, width - most)),
         ],
         "scatter": [
             ("recv", recv_up, (0, width)),
-            ("send", send_up, (0, half)),
-            ("send", late_first, (half, half)),
+            ("send", send_up, (0, most)),
+            ("send", late_first, (most, width - most)),
         ],
         "total": [
             (recv_moves + send_moves, (0, half), 0),
-            (recv_moves[:1] + send_moves + recv_moves[1:], (half, half), 0),
+            (recv_moves + send_moves, (half, half), 0),
             (recv_moves + send_moves, (0, half), 2 * width),
             (recv_moves[:1] + send_moves + recv_moves[1:], (half, half), 2 * width),
         ],
@@ -443,9 +464,6 @@
     recv_count = lax.axis_size("recv")
     send_count = lax.axis_size("send")
     recv_bits, send_bits = bits_of(recv_count), bits_of(send_count)
-    recv_index = lax.axis_index("recv")
-    recv_local = receivers - recv_index * (send_count * node_rows)
-    send_local = senders // node_rows // send_count * node_rows + senders % node_rows
     plan = make_plan(recv_bits, send_bits, width)
     factor = 1.0 / math.sqrt(slot_count * recv_count * send_count)
     vmem = pl.BlockSpec(memory_space=pltpu.VMEM)
@@ -467,20 +485,25 @@
         copies += 2 * len(order)
     moves = len(plan["moves"])
     copies += moves
-    edge_out, send_grad, recv_grad, weights, small = pl.pallas_call(
+    return pl.pallas_call(
         functools.partial(whole_kernel, plan, factor),
         out_shape=(
             f32(slot_count, width),
             f32(node_rows, width),
             f32(node_rows, width),
-            f32(4 * width, width),
-            f32(8, width),
+            f32(3 * width, width),
+            f32(width, width),
+            f32(4, width),
         ),
-        in_specs=[smem, vmem, anywhere, anywhere, vmem, vmem, vmem, vmem, anywhere, vmem, anywhere, vmem, vmem],
-        out_specs=(vmem,) * 5,
+        in_specs=[smem, vmem, anywhere, anywhere, vmem, vmem, anywhere, vmem, anywhere, vmem, vmem],
+        out_specs=(anywhere, vmem, vmem, anywhere, anywhere, vmem),
         scratch_shapes=[
             pltpu.SemaphoreType.DMA((2, copies)),
             pltpu.SemaphoreType.DMA((4,)),
+            pltpu.VMEM((slot_count, width), jnp.float32),
+            pltpu.VMEM((4 * width, width), jnp.float32),
+            pltpu.VMEM((slot_count, 128), jnp.int32),
+            pltpu.VMEM((slot_count, 128), jnp.int32),
             pltpu.VMEM((slot_count, width), jnp.float32),
             pltpu.VMEM((slot_count, width), jnp.float32),
             pltpu.VMEM((4 * width, width), half_type),
@@ -503,17 +526,14 @@
         latent,
         edge_feat,
         cotangent,
-        send_local[:, None],
-        send_local[None, :],
-        recv_local[:, None],
-        recv_local[None, :],
+        senders[None, :],
+        receivers[None, :],
         w_first,
         first_bias[None, :],
         w_second,
         second_bias[None, :],
         norm_gain[None, :],
     )
-    return (edge_out, send_grad, recv_grad, weights[width:], weights[:width], small[:4])
 
 
 def solution(mesh):

time: 146 us -> 152 us (1.041)
  Pallas kernels: 130 us -> 142 us
  local copies, waits for them, and re-layouts: 12.4 us -> 8.19 us
    pallas_call x1, Pallas kernels: 130 us -> 142 us  [shards(): pl.pallas_call(functools.partial(whole_kernel, plan, factor), out_shape=(...]
    slice x3 -> x0, local copies, waits for them, and re-layouts: 7.59 us -> none  [the longest x1 4.01 us: shards(): weights[width:]]
    unnamed x13 -> x16, local copies, waits for them, and re-layouts: 2.74 us -> 8.19 us
    broadcast_in_dim x2 -> x0, local copies, waits for them, and re-layouts: 2.05 us -> none  [the longest x1 1.03 us: shards(): send_local[:, None]]
where the time goes in v3:
time: 152 us
  Pallas kernels  142 us (93%)
  local copies, waits for them, and re-layouts  8.19 us (5%)
    pallas_call x1, Pallas kernels, shards(): pl.pallas_call(functools.partial(whole_kernel, plan, factor), out_shape=(...  142 us
    unnamed x16, local copies, waits for them, and re-layouts  8.19 us

profile of v3, /device:TPU:0, one launch (start us, length us, event | category | flops | bytes accessed | tf_op | source)
XLA Modules:
  0.0 151.7 jit_solution(900174931626200784)
XLA Ops:
  1.3 142.2 %edge_block.1 = (f32[1024,512]{1,0:T(8,128)}, f32[128,512]{1,0:T(8,128)}, f32[128,512]{1,0:T(8,128)}, f32[1536,512]{1,0:T(8,128)}, f32[512,512]{1,0:T(8,128)}, /*index=5*/f32[4,512]{1,0:T(4,128)}) custom-call(s32[1]{0:T(128)S(6)} %copy.23.live_ref, f32[128,512]{1,0:T(8,128)} %latent_ref.1, f32[1024,512]{1,0:T(8,128)} %edge_hbm.1, f32[1024,512]{1,0:T(8,128)} %cot_hbm.1, ...), custom_call_target="tpu_custom_call" | custom-call | tf_op jit(solution)/shard_map/edge_block/pallas_call | solution.py:488
  143.5 0.0 copy-start.3
  143.5 0.0 copy-start.2
  143.5 0.0 copy-start
  143.5 3.2 %copy.24 = f32[1024,512]{1,0:T(8,128)} copy(f32[1024,512]{1,0:T(8,128)} %get-tuple-element.12) | data formatting | bytes 4194304
  146.8 0.0 copy-done.3
  146.8 0.7 copy.25
  147.5 0.0 copy-done.2
  147.5 0.7 copy.26
  148.2 0.0 copy-done
  148.2 0.0 copy-start.1
  148.2 1.7 %copy.27 = f32[1536,512]{1,0:T(8,128)} copy(f32[1536,512]{1,0:T(8,128)S(1)} %copy-done) | data formatting | bytes 6291456
  149.8 0.3 copy-done.1
  150.1 0.0 copy-start.4
  150.1 1.0 copy.28
  151.1 0.0 copy-done.4
  151.1 0.6 copy.29
Async XLA Ops:
  143.5 3.3 %copy-start.3 = (f32[128,512]{1,0:T(8,128)S(1)}, f32[128,512]{1,0:T(8,128)}, u32[]{:S(2)}) copy-start(f32[128,512]{1,0:T(8,128)} %get-tuple-element.13) | copy-start | bytes 786436
  143.5 4.0 %copy-start.2 = (f32[128,512]{1,0:T(8,128)S(1)}, f32[128,512]{1,0:T(8,128)}, u32[]{:S(2)}) copy-start(f32[128,512]{1,0:T(8,128)} %get-tuple-element.14) | copy-start | bytes 786436
  143.5 4.7 %copy-start = (f32[1536,512]{1,0:T(8,128)S(1)}, f32[1536,512]{1,0:T(8,128)}, u32[]{:S(2)}) copy-start(f32[1536,512]{1,0:T(8,128)} %get-tuple-element.15) | copy-start | bytes 9437188
  148.2 2.0 %copy-start.1 = (f32[512,512]{1,0:T(8,128)S(1)}, f32[512,512]{1,0:T(8,128)}, u32[]{:S(2)}) copy-start(f32[512,512]{1,0:T(8,128)} %get-tuple-element.16) | copy-start | bytes 3145732
  150.1 1.0 copy-start.4

commit v4 on v3

--- a/solution.py
+++ b/solution.py
@@ -391,6 +391,8 @@
     edge_store = pltpu.make_async_copy(edge_out, edge_hbm_out, local_sems.at[2])
 
     def finish():
+        yield
+
         def edge_back(i):
             at = rows_at(i)
             edge_out[at, :] = cot_ref[at, :] + dot3(split(edge_out[at, :]), (wh[part[1], :], wl[part[1], :]), NT)
@@ -399,7 +401,7 @@
         edge_store.start()
         yield
 
-    run_streams(early + late + [small, finish()] + scatters)
+    run_streams(scatters + early + late + [small, finish()])
     stores = [
         pltpu.make_async_copy(g_out.at[part[0]], w2_hbm_out, local_sems.at[0]),
         pltpu.make_async_copy(g_out.at[pl.ds(width, 3 * width)], w1_hbm_out, local_sems.at[1]),
@@ -418,7 +420,7 @@
 
 def make_plan(recv_bits, send_bits, width):
     half = width // 2
-    most = width // 4 * 3
+    most = width // 2
     recv_up = list(range(recv_bits))
     send_up = list(range(send_bits))
     recv_down, send_down = recv_up[::-1], send_up[::-1]
@@ -439,7 +441,7 @@
         ],
         "total": [
             (recv_moves + send_moves, (0, half), 0),
-            (recv_moves + send_moves, (half, half), 0),
+            (recv_moves[:1] + send_moves + recv_moves[1:], (half, half), 0),
             (recv_moves + send_moves, (0, half), 2 * width),
             (recv_moves[:1] + send_moves + recv_moves[1:], (half, half), 2 * width),
         ],

time: 152 us -> 138 us (0.908)
  Pallas kernels: 142 us -> 129 us
    pallas_call x1, Pallas kernels: 142 us -> 129 us  [shards(): pl.pallas_call(functools.partial(whole_kernel, plan, factor), out_shape=(...]
where the time goes in v4:
time: 138 us
  Pallas kernels  129 us (93%)
  local copies, waits for them, and re-layouts  8.19 us (6%)
    pallas_call x1, Pallas kernels, shards(): pl.pallas_call(functools.partial(whole_kernel, plan, factor), out_shape=(...  129 us
    unnamed x16, local copies, waits for them, and re-layouts  8.19 us

profile of v4, /device:TPU:0, one launch (start us, length us, event | category | flops | bytes accessed | tf_op | source)
XLA Modules:
  0.0 138.1 jit_solution(1175455860714404232)
XLA Ops:
  1.3 128.6 %edge_block.1 = (f32[1024,512]{1,0:T(8,128)}, f32[128,512]{1,0:T(8,128)}, f32[128,512]{1,0:T(8,128)}, f32[1536,512]{1,0:T(8,128)}, f32[512,512]{1,0:T(8,128)}, /*index=5*/f32[4,512]{1,0:T(4,128)}) custom-call(s32[1]{0:T(128)S(6)} %copy.23.live_ref, f32[128,512]{1,0:T(8,128)} %latent_ref.1, f32[1024,512]{1,0:T(8,128)} %edge_hbm.1, f32[1024,512]{1,0:T(8,128)} %cot_hbm.1, ...), custom_call_target="tpu_custom_call" | custom-call | tf_op jit(solution)/shard_map/edge_block/pallas_call | solution.py:490
  129.9 0.0 copy-start.3
  129.9 0.0 copy-start.2
  129.9 0.0 copy-start
  129.9 3.2 %copy.24 = f32[1024,512]{1,0:T(8,128)} copy(f32[1024,512]{1,0:T(8,128)} %get-tuple-element.12) | data formatting | bytes 4194304
  133.2 0.0 copy-done.3
  133.2 0.7 copy.25
  133.9 0.0 copy-done.2
  133.9 0.7 copy.26
  134.6 0.0 copy-done
  134.6 0.0 copy-start.1
  134.6 1.7 %copy.27 = f32[1536,512]{1,0:T(8,128)} copy(f32[1536,512]{1,0:T(8,128)S(1)} %copy-done) | data formatting | bytes 6291456
  136.2 0.3 copy-done.1
  136.5 0.0 copy-start.4
  136.5 1.0 copy.28
  137.5 0.0 copy-done.4
  137.5 0.6 copy.29
Async XLA Ops:
  129.9 3.3 %copy-start.3 = (f32[128,512]{1,0:T(8,128)S(1)}, f32[128,512]{1,0:T(8,128)}, u32[]{:S(2)}) copy-start(f32[128,512]{1,0:T(8,128)} %get-tuple-element.13) | copy-start | bytes 786436
  129.9 4.0 %copy-start.2 = (f32[128,512]{1,0:T(8,128)S(1)}, f32[128,512]{1,0:T(8,128)}, u32[]{:S(2)}) copy-start(f32[128,512]{1,0:T(8,128)} %get-tuple-element.14) | copy-start | bytes 786436
  129.9 4.7 %copy-start = (f32[1536,512]{1,0:T(8,128)S(1)}, f32[1536,512]{1,0:T(8,128)}, u32[]{:S(2)}) copy-start(f32[1536,512]{1,0:T(8,128)} %get-tuple-element.15) | copy-start | bytes 9437188
  134.6 2.0 %copy-start.1 = (f32[512,512]{1,0:T(8,128)S(1)}, f32[512,512]{1,0:T(8,128)}, u32[]{:S(2)}) copy-start(f32[512,512]{1,0:T(8,128)} %get-tuple-element.16) | copy-start | bytes 3145732
  136.5 1.0 copy-start.4
